TPU v7x, 128 devices: a whole 4x4x4 slice. The times are simulated.
128 devices in a mesh: sx: 8 (over y, core), sy: 16 (over x, z).
Axes of the slice: x: 4, y: 4, z: 4, core: 2. Of those that a mesh axis runs over, the one named last changes fastest.
Arguments:
- loads: float32 [8, 16, 1536, 256], P('sx', 'sy')
- schur_flex: float32 [8, 16, 1536, 1536], P('sx', 'sy'), as said below
- dirichlet: float32 [8, 16, 1536, 1536], P('sx', 'sy'), as said below
- coupling: float32 [8, 16, 16, 1536], P('sx', 'sy'), may hold values from -0.3125 to 0.3125
- corner_index: int32 [8, 16, 16], P('sx', 'sy'), may hold values from 0 to 512, as said below
- face_lists: int32 [8, 16, 4, 384], P('sx', 'sy'), may hold values from 0 to 383, as said below
- coarse_inverse: float32 [512, 512], P(('sx', 'sy')), as said below
Outputs:
- multipliers: float32 [8, 16, 1536, 256], P('sx', 'sy')
- residual: float32 [8, 16, 1536, 256], P('sx', 'sy')
Inputs may be any that keep to these rules, and one draw needn't show every extreme that they name: `corner_index`: each subdomain lists 4 coarse dofs for each of its four corners; 512 marks a corner on the clamped edges of the panel, which has no coarse dof; every coarse dof below 512 is named by some subdomain. `face_lists`: each face's list is a permutation of the 384 dofs of the facing face; the facing lists of two neighbouring subdomains are inverse permutations. `schur_flex`: symmetric positive definite for every subdomain. `dirichlet`: symmetric positive definite for every subdomain. `coarse_inverse`: symmetric positive definite.
All inputs are finite; a program needn't handle non-finite values.
Results may differ from a plain program's by a relative error of at most 0.00017.
Values sent between devices are 32-bit elements; how exact they have to be, the bound alone decides.
A program may use at most 128 MiB of HBM per device.

v0:
```python
import jax
import jax.numpy as jnp
from jax import lax
from jax.sharding import PartitionSpec as P

ITERS = 2


def shifted(block, axis, distance):
    devices = range(lax.axis_size(axis))
    route = [(i - distance, i) for i in devices if i - distance in devices]
    return lax.ppermute(block, axis, route)


def jump(field, face_index):
    size = field.shape[0] // 4
    width = field.shape[1]
    face_rows = field.reshape(4, size, width)
    from_low_x = shifted(face_rows[1], "sx", 1)
    from_high_x = shifted(face_rows[0], "sx", -1)
    from_low_y = shifted(face_rows[3], "sy", 1)
    from_high_y = shifted(face_rows[2], "sy", -1)
    received = jnp.stack([from_low_x, from_high_x, from_low_y, from_high_y], axis=0)
    matched = received[jnp.arange(4, dtype=jnp.int32)[:, None], face_index]
    return (face_rows - matched).reshape(4 * size, width)


def coarse_solve(coarse_rhs, stiffness_inverse_lines):
    highest = lax.Precision.HIGHEST
    total = lax.psum(coarse_rhs, ("sx", "sy"))
    mine = jnp.dot(stiffness_inverse_lines, total, precision=highest)
    return lax.all_gather(mine, ("sx", "sy"), axis=0, tiled=True)


def inner(first, second):
    return jnp.sum(first * second, axis=0)


def shards(loads, schur_flex, dirichlet, coupling, corner_index, face_lists, coarse_inverse):
    highest = lax.Precision.HIGHEST
    flex_mat = schur_flex[0, 0]
    prec_mat = dirichlet[0, 0]
    coupling_mat = coupling[0, 0]
    corners = corner_index[0, 0]
    face_index = face_lists[0, 0]
    ncoarse = coarse_inverse.shape[1]
    onehot = (corners[None, :] == jnp.arange(ncoarse, dtype=jnp.int32)[:, None]).astype(jnp.float32)

    def precondition(dual_vector):
        spread = jump(dual_vector, face_index)
        operator_applied = jnp.dot(prec_mat, spread, precision=highest)
        return 0.5 * jump(operator_applied, face_index)

    def residual_dot(residual, precond):
        return lax.psum(inner(residual, precond), ("sx", "sy"))

    force_discontinuity = jump(loads[0, 0], face_index)
    multipliers = jnp.zeros_like(force_discontinuity)
    residual = force_discontinuity
    precond = precondition(residual)
    direction = precond
    residual_inner = residual_dot(residual, precond)
    for iteration in range(ITERS):
        width = direction.shape[1]
        apply_spread = jump(direction, face_index)
        fine_part = jnp.dot(flex_mat, apply_spread, precision=highest)
        local_load = jnp.dot(coupling_mat, apply_spread, precision=highest)
        coarse_rhs = jnp.dot(onehot, local_load, precision=highest)
        coarse_sol = coarse_solve(coarse_rhs, coarse_inverse)
        filled_out = jnp.concatenate([coarse_sol, jnp.zeros((1, width), jnp.float32)], axis=0)
        picked = filled_out[corners]
        correction = lax.dot_general(
            coupling_mat, picked, (((0,), (0,)), ((), ())), precision=highest
        )
        image_dir = jump(fine_part + correction, face_index)
        step_size = residual_inner / lax.psum(inner(direction, image_dir), ("sx", "sy"))
        multipliers = multipliers + step_size * direction
        residual = residual - step_size * image_dir
        if iteration + 1 < ITERS:
            precond = precondition(residual)
            new_dot = residual_dot(residual, precond)
            direction = precond + new_dot / residual_inner * direction
            residual_inner = new_dot
    return (multipliers[None, None], residual[None, None])


def solution(mesh):
    return jax.shard_map(
        shards,
        mesh=mesh,
        in_specs=(
            P("sx", "sy", None, None),
            P("sx", "sy", None, None),
            P("sx", "sy", None, None),
            P("sx", "sy", None, None),
            P("sx", "sy", None),
            P("sx", "sy", None, None),
            P(("sx", "sy"), None),
        ),
        out_specs=(P("sx", "sy", None, None), P("sx", "sy", None, None)),
        check_vma=False,
    )
```

profile of v0, /device:TPU:1, one launch (start us, length us, event | category | flops | bytes accessed | tf_op | source)
XLA Modules:
  0.0 1103.3 jit_solution(2738854772131072380)
XLA Ops:
  30.4 18.0 %gather_fusion = f32[1536,256]{1,0:T(8,128)} fusion(f32[4,384,256]{2,1,0:T(8,128)S(1)} %pad_maximum_fusion, s32[1536]{0:T(1024)S(1)} %reshape.175), kind=kCustom, calls=%fused_computation | custom fusion | bytes 3158016 | tf_op jit(solution)/shard_map/gather | solution.py:24
  51.4 5.1 collective-permute-start.4
  72.3 18.0 %gather_fusion.1 = f32[1536,256]{1,0:T(8,128)} fusion(f32[4,384,256]{2,1,0:T(8,128)S(1)} %pad_maximum_fusion.1, s32[1536]{0:T(1024)S(1)} %reshape.175), kind=kCustom, calls=%fused_computation.1 | custom fusion | bytes 3158016 | tf_op jit(solution)/shard_map/gather | solution.py:24
  92.1 18.2 %fusion.10 = f32[1536,256]{0,1:T(8,128)S(1)} fusion(f32[1536,256]{1,0:T(8,128)S(1)} %bitcast.126, f32[1,1,1536,1536]{3,2,1,0:T(8,128)} %param.9), kind=kOutput, calls=%fused_computation.23 | convolution fusion | flops 7247757312 | bytes 12582912 | tf_op jit(solution)/shard_map/dot_general | solution.py:51
  110.3 5.9 collective-permute-start.8
  134.2 18.0 %gather_fusion.2 = f32[1536,256]{1,0:T(8,128)} fusion(f32[4,384,256]{2,1,0:T(8,128)S(1)} %copy.27, s32[1536]{0:T(1024)S(1)} %reshape.175), kind=kCustom, calls=%fused_computation.2 | custom fusion | bytes 3158016 | tf_op jit(solution)/shard_map/gather | solution.py:24
  157.2 6.4 collective-permute-start.12
  181.3 18.0 %gather_fusion.3 = f32[1536,256]{1,0:T(8,128)} fusion(f32[4,384,256]{2,1,0:T(8,128)S(1)} %copy.31, s32[1536]{0:T(1024)S(1)} %reshape.175), kind=kCustom, calls=%fused_computation.3 | custom fusion | bytes 3158016 | tf_op jit(solution)/shard_map/gather | solution.py:24
  203.9 11.6 %fusion.2 = f32[256,1536]{1,0:T(8,128)} fusion(f32[1,1,1536,1536]{3,2,1,0:T(8,128)} %param.8, f32[1536,256]{0,1:T(8,128)S(1)} %copy.32, f32[1536,256]{0,1:T(8,128)S(1)} %get-tuple-element.16), kind=kOutput, calls=%fused_computation.13 | convolution fusion | flops 7248543744 | bytes 14155776 | tf_op jit(solution)/shard_map/dot_general | solution.py:66
  215.4 139.1 %all-reduce.6.cloned.1.call-done = f32[512,256]{1,0:T(8,128)} async-done(((f32[512,256]{1,0:T(8,128)}), f32[512,256]{1,0:T(8,128)}) %all-reduce.6.cloned.1.call-update) | async-done | bytes 524304 | tf_op jit(solution)/shard_map/psum | solution.py:30
  355.9 54.6 %all-gather = f32[128,4,256]{2,1,0:T(4,128)} all-gather(f32[1,4,256]{2,1,0:T(4,128)S(1)} %convolution_bitcast_fusion.1), channel_id=1, replica_groups=mesh['sx'=8,'sy'=16] {'sx','sy'}, dimensions={0}, use_global_device_ids=true | all-gather | bytes 528384 | tf_op jit(solution)/shard_map/all_gather | solution.py:32
  435.2 4.9 collective-permute-done.19
  444.6 18.0 %gather_fusion.5 = f32[1536,256]{1,0:T(8,128)} fusion(f32[4,384,256]{2,1,0:T(8,128)S(1)} %copy.33, s32[1536]{0:T(1024)S(1)} %reshape.175), kind=kCustom, calls=%fused_computation.5 | custom fusion | bytes 3158016 | tf_op jit(solution)/shard_map/gather | solution.py:24
  469.6 66.2 %all-reduce.2 = (f32[256]{0:T(256)S(1)}, f32[256]{0:T(256)S(1)}) all-reduce(f32[256]{0:T(256)S(1)} %get-tuple-element.7, f32[256]{0:T(256)S(1)} %get-tuple-element.6), channel_id=1, replica_groups=mesh['sx'=8,'sy'=16] {'sx','sy'}, use_global_device_ids=true, to_apply=%region_1.0 | all-reduce | flops 512 | bytes 4096 | tf_op jit(solution)/shard_map/psum | solution.py:55
  562.5 18.0 %gather_fusion.6 = f32[1536,256]{1,0:T(8,128)} fusion(f32[4,384,256]{2,1,0:T(8,128)S(1)} %copy.35, s32[1536]{0:T(1024)S(1)} %reshape.175), kind=kCustom, calls=%fused_computation.6 | custom fusion | bytes 3158016 | tf_op jit(solution)/shard_map/gather | solution.py:24
  583.7 11.3 %fusion.13 = f32[1536,256]{0,1:T(8,128)S(1)} fusion(f32[1,1,1536,1536]{3,2,1,0:T(8,128)} %param.9, f32[1536,256]{0,1:T(8,128)S(1)} %copy-done.5, f32[1536,256]{0,1:T(8,128)} %copy.36), kind=kOutput, calls=%fused_computation.24 | convolution fusion | flops 7248150528 | bytes 14155776 | tf_op jit(solution)/shard_map/dot_general | solution.py:51
  618.8 18.0 %gather_fusion.7 = f32[1536,256]{1,0:T(8,128)} fusion(f32[4,384,256]{2,1,0:T(8,128)S(1)} %copy.37, s32[1536]{0:T(1024)S(1)} %reshape.175), kind=kCustom, calls=%fused_computation.7 | custom fusion | bytes 3158016 | tf_op jit(solution)/shard_map/gather | solution.py:24
  642.2 69.1 %psum.45 = f32[256]{0:T(256)S(1)} all-reduce(f32[256]{0:T(256)S(1)} %multiply_reduce_fusion.1), channel_id=1, replica_groups=mesh['sx'=8,'sy'=16] {'sx','sy'}, use_global_device_ids=true, to_apply=%region_6.0 | all-reduce | flops 256 | bytes 2048 | tf_op jit(solution)/shard_map/psum | solution.py:55
  737.0 18.0 %gather_fusion.8 = f32[1536,256]{1,0:T(8,128)} fusion(f32[4,384,256]{2,1,0:T(8,128)S(1)} %copy.39, s32[1536]{0:T(1024)S(1)} %reshape.175), kind=kCustom, calls=%fused_computation.8 | custom fusion | bytes 3158016 | tf_op jit(solution)/shard_map/gather | solution.py:24
  762.1 12.2 %fusion = f32[256,1536]{1,0:T(8,128)} fusion(f32[1,1,1536,1536]{3,2,1,0:T(8,128)} %param.8, f32[1536,256]{0,1:T(8,128)S(1)} %copy-done.2, f32[1536,256]{0,1:T(8,128)} %copy.40), kind=kOutput, calls=%fused_computation.11 | convolution fusion | flops 7248150528 | bytes 14155776 | tf_op jit(solution)/shard_map/dot_general | solution.py:66
  774.3 135.6 %all-reduce.8.cloned.1.call-done = f32[512,256]{1,0:T(8,128)} async-done(((f32[512,256]{1,0:T(8,128)}), f32[512,256]{1,0:T(8,128)}) %all-reduce.8.cloned.1.call-update) | async-done | bytes 524304 | tf_op jit(solution)/shard_map/psum | solution.py:30
  911.3 54.2 %all-gather.1 = f32[128,4,256]{2,1,0:T(4,128)} all-gather(f32[1,4,256]{2,1,0:T(4,128)S(1)} %convolution_bitcast_fusion), channel_id=1, replica_groups=mesh['sx'=8,'sy'=16] {'sx','sy'}, dimensions={0}, use_global_device_ids=true | all-gather | bytes 528384 | tf_op jit(solution)/shard_map/all_gather | solution.py:32
  995.9 18.0 %gather_fusion.10 = f32[1536,256]{1,0:T(8,128)} fusion(f32[4,384,256]{2,1,0:T(8,128)S(1)} %copy.41, s32[1536]{0:T(1024)S(1)} %reshape.175), kind=kCustom, calls=%fused_computation.10 | custom fusion | bytes 3158016 | tf_op jit(solution)/shard_map/gather | solution.py:24
  1020.4 66.7 %psum.47 = f32[256]{0:T(256)S(1)} all-reduce(f32[256]{0:T(256)S(1)} %get-tuple-element.12), channel_id=1, replica_groups=mesh['sx'=8,'sy'=16] {'sx','sy'}, use_global_device_ids=true, to_apply=%region_9.0 | all-reduce | flops 256 | bytes 2048 | tf_op jit(solution)/shard_map/psum | solution.py:76
  (180 shorter events, 264.9 us)
Async XLA Ops:
  7.2 347.3 %all-reduce.6.cloned.1.call-start = ((), (), s32[]{:S(2)}) async-start(), calls=%async_computation | async-start | bytes 1048576 | tf_op jit(solution)/shard_map/psum | solution.py:30
  8.7 11.4 %collective-permute-start = (f32[384,256]{1,0:T(8,128)S(1)}, f32[384,256]{1,0:T(8,128)S(1)}, u32[]{:S(2)}, u32[]{:S(2)}) collective-permute-start(f32[384,256]{1,0:T(8,128)S(1)} %get-tuple-element.49), channel_id=1, source_target_pairs={{0,16},{16,32},{32,48},{48,64},{64,80},{80,96},{96,112},{1,17},{17... | collective-permute-start | bytes 1179656 | tf_op jit(solution)/shard_map/ppermute | solution.py:12
  13.3 9.4 collective-permute-start.1
  15.2 11.0 collective-permute-start.2
  18.8 11.5 %collective-permute-start.3 = (f32[384,256]{1,0:T(8,128)S(1)}, f32[384,256]{1,0:T(8,128)S(1)}, u32[]{:S(2)}, u32[]{:S(2)}) collective-permute-start(f32[384,256]{1,0:T(8,128)S(1)} %get-tuple-element.52), channel_id=1, source_target_pairs={{1,0},{2,1},{3,2},{4,3},{5,4},{6,5},{7,6},{8,7},{9,8},{10,9},{11,1... | collective-permute-start | bytes 1179656 | tf_op jit(solution)/shard_map/ppermute | solution.py:12
  51.4 11.8 %collective-permute-start.4 = (f32[384,256]{1,0:T(8,128)S(1)}, f32[384,256]{1,0:T(8,128)S(1)}, u32[]{:S(2)}, u32[]{:S(2)}) collective-permute-start(f32[384,256]{1,0:T(8,128)S(1)} %get-tuple-element.45), channel_id=1, source_target_pairs={{0,16},{16,32},{32,48},{48,64},{64,80},{80,96},{96,112},{1,17},{17... | collective-permute-start | bytes 1179656 | tf_op jit(solution)/shard_map/ppermute | solution.py:12
  58.5 9.6 collective-permute-start.6
  61.9 10.3 collective-permute-start.7
  110.3 13.3 %collective-permute-start.8 = (f32[384,256]{0,1:T(8,128)S(1)}, f32[384,256]{0,1:T(8,128)S(1)}, u32[]{:S(2)}, u32[]{:S(2)}) collective-permute-start(f32[384,256]{0,1:T(8,128)S(1)} %get-tuple-element.41), channel_id=1, source_target_pairs={{0,16},{16,32},{32,48},{48,64},{64,80},{80,96},{96,112},{1,17},{17... | collective-permute-start | bytes 1179656 | tf_op jit(solution)/shard_map/ppermute | solution.py:12
  116.3 9.4 collective-permute-start.9
  157.2 13.8 %collective-permute-start.12 = (f32[384,256]{0,1:T(8,128)S(1)}, f32[384,256]{0,1:T(8,128)S(1)}, u32[]{:S(2)}, u32[]{:S(2)}) collective-permute-start(f32[384,256]{0,1:T(8,128)S(1)} %get-tuple-element.37), channel_id=1, source_target_pairs={{0,16},{16,32},{32,48},{48,64},{64,80},{80,96},{96,112},{1,17},{17... | collective-permute-start | bytes 1179656 | tf_op jit(solution)/shard_map/ppermute | solution.py:12
  203.8 706.1 %all-reduce.8.cloned.1.call-start = ((), (), s32[]{:S(2)}) async-start(), calls=%async_computation.1 | async-start | bytes 1048576 | tf_op jit(solution)/shard_map/psum | solution.py:30
  419.1 13.7 %collective-permute-start.16 = (f32[384,256]{0,1:T(8,128)}, f32[384,256]{0,1:T(8,128)}, u32[]{:S(2)}, u32[]{:S(2)}) collective-permute-start(f32[384,256]{0,1:T(8,128)} %get-tuple-element.33), channel_id=1, source_target_pairs={{0,16},{16,32},{32,48},{48,64},{64,80},{80,96},{96,112},{1,17},{17... | collective-permute-start | bytes 1179656 | tf_op jit(solution)/shard_map/ppermute | solution.py:12
  421.0 11.8 %collective-permute-start.17 = (f32[384,256]{0,1:T(8,128)}, f32[384,256]{0,1:T(8,128)}, u32[]{:S(2)}, u32[]{:S(2)}) collective-permute-start(f32[384,256]{0,1:T(8,128)} %get-tuple-element.36), channel_id=1, source_target_pairs={{16,0},{32,16},{48,32},{64,48},{80,64},{96,80},{112,96},{17,1},{33... | collective-permute-start | bytes 1179656 | tf_op jit(solution)/shard_map/ppermute | solution.py:12
  424.2 11.1 %collective-permute-start.18 = (f32[384,256]{0,1:T(8,128)}, f32[384,256]{0,1:T(8,128)}, u32[]{:S(2)}, u32[]{:S(2)}) collective-permute-start(f32[384,256]{0,1:T(8,128)} %get-tuple-element.35), channel_id=1, source_target_pairs={{0,1},{1,2},{2,3},{3,4},{4,5},{5,6},{6,7},{7,8},{8,9},{9,10},{10,1... | collective-permute-start | bytes 1179656 | tf_op jit(solution)/shard_map/ppermute | solution.py:12
  426.9 13.2 %collective-permute-start.19 = (f32[384,256]{0,1:T(8,128)}, f32[384,256]{0,1:T(8,128)}, u32[]{:S(2)}, u32[]{:S(2)}) collective-permute-start(f32[384,256]{0,1:T(8,128)} %get-tuple-element.34), channel_id=1, source_target_pairs={{1,0},{2,1},{3,2},{4,3},{5,4},{6,5},{7,6},{8,7},{9,8},{10,9},{11,1... | collective-permute-start | bytes 1179656 | tf_op jit(solution)/shard_map/ppermute | solution.py:12
  542.9 9.4 collective-permute-start.21
  544.8 10.5 collective-permute-start.22
  546.5 12.9 %collective-permute-start.23 = (f32[384,256]{0,1:T(8,128)S(1)}, f32[384,256]{0,1:T(8,128)S(1)}, u32[]{:S(2)}, u32[]{:S(2)}) collective-permute-start(f32[384,256]{0,1:T(8,128)S(1)} %get-tuple-element.30), channel_id=1, source_target_pairs={{1,0},{2,1},{3,2},{4,3},{5,4},{6,5},{7,6},{8,7},{9,8},{10,9},{11,1... | collective-permute-start | bytes 1179656 | tf_op jit(solution)/shard_map/ppermute | solution.py:12
  601.5 9.9 collective-permute-start.26
  603.8 11.8 %collective-permute-start.27 = (f32[384,256]{0,1:T(8,128)S(1)}, f32[384,256]{0,1:T(8,128)S(1)}, u32[]{:S(2)}, u32[]{:S(2)}) collective-permute-start(f32[384,256]{0,1:T(8,128)S(1)} %get-tuple-element.26), channel_id=1, source_target_pairs={{1,0},{2,1},{3,2},{4,3},{5,4},{6,5},{7,6},{8,7},{9,8},{10,9},{11,1... | collective-permute-start | bytes 1179656 | tf_op jit(solution)/shard_map/ppermute | solution.py:12
  722.1 11.7 %collective-permute-start.31 = (f32[384,256]{0,1:T(8,128)S(1)}, f32[384,256]{0,1:T(8,128)S(1)}, u32[]{:S(2)}, u32[]{:S(2)}) collective-permute-start(f32[384,256]{0,1:T(8,128)S(1)} %get-tuple-element.22), channel_id=1, source_target_pairs={{1,0},{2,1},{3,2},{4,3},{5,4},{6,5},{7,6},{8,7},{9,8},{10,9},{11,1... | collective-permute-start | bytes 1179656 | tf_op jit(solution)/shard_map/ppermute | solution.py:12
  977.9 10.7 collective-permute-start.34
  979.9 12.9 %collective-permute-start.35 = (f32[384,256]{0,1:T(8,128)S(1)}, f32[384,256]{0,1:T(8,128)S(1)}, u32[]{:S(2)}, u32[]{:S(2)}) collective-permute-start(f32[384,256]{0,1:T(8,128)S(1)} %get-tuple-element.18), channel_id=1, source_target_pairs={{1,0},{2,1},{3,2},{4,3},{5,4},{6,5},{7,6},{8,7},{9,8},{10,9},{11,1... | collective-permute-start | bytes 1179656 | tf_op jit(solution)/shard_map/ppermute | solution.py:12
  (35 other events, 967.1 us)
Sparse Core Ops, SparseCore 0:
  203.9 150.5 all-reduce.5
  762.2 147.6 all-reduce.7
where the time goes:
time: 1110 us; the launch traced here: 1100 us
  waiting for transfers between devices  359 us (32%)
  blocking collectives  311 us (28%)
  local copies, waits for them, and re-layouts  225 us (20%)
  starting transfers between devices  93.2 us (8%)
  matrix products  65.3 us (6%)
  other arithmetic  34.2 us (3%)
  between operations  15.2 us (1%)
    psum x2, waiting for transfers between devices, coarse_solve(): total = lax.psum(coarse_rhs, ('sx', 'sy'))  275 us
    gather x17, local copies, waits for them, and re-layouts, jump(): matched = received[jnp.arange(4, dtype=jnp.int32)[:, None], face_index]  186 us
    psum x2, blocking collectives, residual_dot(): return lax.psum(inner(residual, precond), ('sx', 'sy'))  135 us
    all_gather x2, blocking collectives, coarse_solve(): return lax.all_gather(mine, ('sx', 'sy'), axis=0, tiled=True)  109 us
    ppermute x36, starting transfers between devices, shifted(): return lax.ppermute(block, axis, route)  93.1 us
    ppermute x36, waiting for transfers between devices, shifted(): return lax.ppermute(block, axis, route)  84.4 us
    psum x1, blocking collectives, shards(): lax.psum(inner(direction, image_dir), ('sx', 'sy'))  66.7 us
    dot_general x2, matrix products, precondition(): operator_applied = jnp.dot(prec_mat, spread, precision=highest)  29.5 us
  transfers between devices with their start and end apart: 38, of which 28 were waited for; matrix products, arithmetic and copies ran while one was open for 3% of the time, Pallas kernels for 0%

commit v1 on v0

--- a/solution.py
+++ b/solution.py
@@ -29,7 +29,15 @@
     highest = lax.Precision.HIGHEST
     total = lax.psum(coarse_rhs, ("sx", "sy"))
     mine = jnp.dot(stiffness_inverse_lines, total, precision=highest)
-    return lax.all_gather(mine, ("sx", "sy"), axis=0, tiled=True)
+    return jnp.concatenate(
+        lax.all_to_all(
+            jnp.stack(lax.psum(1, ("sx", "sy")) * [mine], 0),
+            ("sx", "sy"),
+            split_axis=0,
+            concat_axis=0,
+        ),
+        0,
+    )
 
 
 def inner(first, second):

time: 1110 us -> 1050 us (0.946)
  blocking collectives: 311 us -> 200 us
  waiting for transfers between devices: 359 us -> 384 us
  starting transfers between devices: 93.2 us -> 110 us
    all_gather x2 -> x0, blocking collectives: 109 us -> none  [coarse_solve(): return lax.all_gather(mine, ('sx', 'sy'), axis=0, tiled=True)]
    psum x2, waiting for transfers between devices: 275 us -> 298 us  [coarse_solve(): total = lax.psum(coarse_rhs, ('sx', 'sy'))]
    all_to_all x0 -> x2, starting transfers between devices: none -> 14.5 us  [coarse_solve(): lax.all_to_all(jnp.stack(lax.psum(1, ('sx', 'sy')) * [mine], 0), ('sx', '...]
  transfers between devices with their start and end apart: 38 -> 40, of which waited for: 28 -> 30; matrix products, arithmetic and copies ran while one was open for 3% -> 3% of each run, Pallas kernels for 0% -> 0%
where the time goes in v1:
time: 1050 us; the launch traced here: 1040 us
  waiting for transfers between devices  384 us (37%)
  local copies, waits for them, and re-layouts  227 us (22%)
  blocking collectives  200 us (19%)
  starting transfers between devices  110 us (10%)
  matrix products  65.3 us (6%)
  other arithmetic  34.2 us (3%)
  between operations  15.3 us (1%)
    psum x2, waiting for transfers between devices, coarse_solve(): total = lax.psum(coarse_rhs, ('sx', 'sy'))  298 us
    gather x17, local copies, waits for them, and re-layouts, jump(): matched = received[jnp.arange(4, dtype=jnp.int32)[:, None], face_index]  186 us
    psum x2, blocking collectives, residual_dot(): return lax.psum(inner(residual, precond), ('sx', 'sy'))  134 us
    ppermute x36, starting transfers between devices, shifted(): return lax.ppermute(block, axis, route)  95.5 us
    ppermute x36, waiting for transfers between devices, shifted(): return lax.ppermute(block, axis, route)  83.9 us
    psum x1, blocking collectives, shards(): lax.psum(inner(direction, image_dir), ('sx', 'sy'))  66.3 us
    dot_general x2, matrix products, precondition(): operator_applied = jnp.dot(prec_mat, spread, precision=highest)  29.5 us
    dot_general x2, matrix products, shards(): fine_part = jnp.dot(flex_mat, apply_spread, precision=highest)  23.7 us
  transfers between devices with their start and end apart: 40, of which 30 were waited for; matrix products, arithmetic and copies ran while one was open for 3% of the time, Pallas kernels for 0%

profile of v1, /device:TPU:1, one launch (start us, length us, event | category | flops | bytes accessed | tf_op | source)
XLA Modules:
  0.0 1036.5 jit_solution(4278924639344781474)
XLA Ops:
  30.4 18.0 %gather_fusion = f32[1536,256]{1,0:T(8,128)} fusion(f32[4,384,256]{2,1,0:T(8,128)S(1)} %pad_maximum_fusion, s32[1536]{0:T(1024)S(1)} %reshape.187), kind=kCustom, calls=%fused_computation | custom fusion | bytes 3158016 | tf_op jit(solution)/shard_map/gather | solution.py:24
  51.4 5.1 collective-permute-start.4
  72.3 18.0 %gather_fusion.1 = f32[1536,256]{1,0:T(8,128)} fusion(f32[4,384,256]{2,1,0:T(8,128)S(1)} %pad_maximum_fusion.1, s32[1536]{0:T(1024)S(1)} %reshape.187), kind=kCustom, calls=%fused_computation.1 | custom fusion | bytes 3158016 | tf_op jit(solution)/shard_map/gather | solution.py:24
  92.1 18.2 %fusion.10 = f32[1536,256]{0,1:T(8,128)S(1)} fusion(f32[1536,256]{1,0:T(8,128)S(1)} %bitcast.122, f32[1,1,1536,1536]{3,2,1,0:T(8,128)} %param.9), kind=kOutput, calls=%fused_computation.23 | convolution fusion | flops 7247757312 | bytes 12582912 | tf_op jit(solution)/shard_map/dot_general | solution.py:59
  110.4 5.9 collective-permute-start.8
  134.2 18.0 %gather_fusion.2 = f32[1536,256]{1,0:T(8,128)} fusion(f32[4,384,256]{2,1,0:T(8,128)S(1)} %copy.9, s32[1536]{0:T(1024)S(1)} %reshape.187), kind=kCustom, calls=%fused_computation.2 | custom fusion | bytes 3158016 | tf_op jit(solution)/shard_map/gather | solution.py:24
  157.2 6.4 collective-permute-start.12
  181.3 18.0 %gather_fusion.3 = f32[1536,256]{1,0:T(8,128)} fusion(f32[4,384,256]{2,1,0:T(8,128)S(1)} %copy.13, s32[1536]{0:T(1024)S(1)} %reshape.187), kind=kCustom, calls=%fused_computation.3 | custom fusion | bytes 3158016 | tf_op jit(solution)/shard_map/gather | solution.py:24
  203.8 150.7 %all-reduce.6.cloned.1.call-done = f32[512,256]{1,0:T(8,128)} async-done(((f32[512,256]{1,0:T(8,128)}), f32[512,256]{1,0:T(8,128)}) %all-reduce.6.cloned.1.call-update) | async-done | bytes 524304 | tf_op jit(solution)/shard_map/psum | solution.py:30
  356.8 7.2 all-to-all-start
  364.5 11.6 %fusion.2 = f32[256,1536]{1,0:T(8,128)} fusion(f32[1,1,1536,1536]{3,2,1,0:T(8,128)} %param.8, f32[1536,256]{0,1:T(8,128)S(1)} %copy.14, f32[1536,256]{0,1:T(8,128)S(1)} %get-tuple-element.14), kind=kOutput, calls=%fused_computation.13 | convolution fusion | flops 7248543744 | bytes 14155776 | tf_op jit(solution)/shard_map/dot_general | solution.py:74
  402.5 5.0 collective-permute-done.19
  412.0 18.0 %gather_fusion.5 = f32[1536,256]{1,0:T(8,128)} fusion(f32[4,384,256]{2,1,0:T(8,128)S(1)} %copy.15, s32[1536]{0:T(1024)S(1)} %reshape.187), kind=kCustom, calls=%fused_computation.5 | custom fusion | bytes 3158016 | tf_op jit(solution)/shard_map/gather | solution.py:24
  437.0 65.6 %all-reduce.2 = (f32[256]{0:T(256)S(1)}, f32[256]{0:T(256)S(1)}) all-reduce(f32[256]{0:T(256)S(1)} %get-tuple-element.5, f32[256]{0:T(256)S(1)} %get-tuple-element.4), channel_id=1, replica_groups=mesh['sx'=8,'sy'=16] {'sx','sy'}, use_global_device_ids=true, to_apply=%region_1.0 | all-reduce | flops 512 | bytes 4096 | tf_op jit(solution)/shard_map/psum | solution.py:63
  528.6 18.0 %gather_fusion.6 = f32[1536,256]{1,0:T(8,128)} fusion(f32[4,384,256]{2,1,0:T(8,128)S(1)} %copy.17, s32[1536]{0:T(1024)S(1)} %reshape.187), kind=kCustom, calls=%fused_computation.6 | custom fusion | bytes 3158016 | tf_op jit(solution)/shard_map/gather | solution.py:24
  549.8 11.3 %fusion.13 = f32[1536,256]{0,1:T(8,128)S(1)} fusion(f32[1,1,1536,1536]{3,2,1,0:T(8,128)} %param.9, f32[1536,256]{0,1:T(8,128)S(1)} %copy-done.5, f32[1536,256]{0,1:T(8,128)} %copy.18), kind=kOutput, calls=%fused_computation.24 | convolution fusion | flops 7248150528 | bytes 14155776 | tf_op jit(solution)/shard_map/dot_general | solution.py:59
  585.8 18.0 %gather_fusion.7 = f32[1536,256]{1,0:T(8,128)} fusion(f32[4,384,256]{2,1,0:T(8,128)S(1)} %copy.19, s32[1536]{0:T(1024)S(1)} %reshape.187), kind=kCustom, calls=%fused_computation.7 | custom fusion | bytes 3158016 | tf_op jit(solution)/shard_map/gather | solution.py:24
  609.2 68.0 %psum.45 = f32[256]{0:T(256)S(1)} all-reduce(f32[256]{0:T(256)S(1)} %multiply_reduce_fusion.1), channel_id=1, replica_groups=mesh['sx'=8,'sy'=16] {'sx','sy'}, use_global_device_ids=true, to_apply=%region_6.0 | all-reduce | flops 256 | bytes 2048 | tf_op jit(solution)/shard_map/psum | solution.py:63
  703.0 17.9 %gather_fusion.8 = f32[1536,256]{1,0:T(8,128)} fusion(f32[4,384,256]{2,1,0:T(8,128)S(1)} %copy.21, s32[1536]{0:T(1024)S(1)} %reshape.187), kind=kCustom, calls=%fused_computation.8 | custom fusion | bytes 3158016 | tf_op jit(solution)/shard_map/gather | solution.py:24
  728.1 147.7 %all-reduce.8.cloned.1.call-done = f32[512,256]{1,0:T(8,128)} async-done(((f32[512,256]{1,0:T(8,128)}), f32[512,256]{1,0:T(8,128)}) %all-reduce.8.cloned.1.call-update) | async-done | bytes 524304 | tf_op jit(solution)/shard_map/psum | solution.py:30
  878.0 7.3 all-to-all-start.1
  885.3 12.2 %fusion = f32[256,1536]{1,0:T(8,128)} fusion(f32[1,1,1536,1536]{3,2,1,0:T(8,128)} %param.8, f32[1536,256]{0,1:T(8,128)S(1)} %copy-done.2, f32[1536,256]{0,1:T(8,128)} %copy.22), kind=kOutput, calls=%fused_computation.11 | convolution fusion | flops 7248150528 | bytes 14155776 | tf_op jit(solution)/shard_map/dot_general | solution.py:74
  929.5 18.0 %gather_fusion.10 = f32[1536,256]{1,0:T(8,128)} fusion(f32[4,384,256]{2,1,0:T(8,128)S(1)} %copy.23, s32[1536]{0:T(1024)S(1)} %reshape.187), kind=kCustom, calls=%fused_computation.10 | custom fusion | bytes 3158016 | tf_op jit(solution)/shard_map/gather | solution.py:24
  954.0 66.3 %psum.47 = f32[256]{0:T(256)S(1)} all-reduce(f32[256]{0:T(256)S(1)} %get-tuple-element.10), channel_id=1, replica_groups=mesh['sx'=8,'sy'=16] {'sx','sy'}, use_global_device_ids=true, to_apply=%region_9.0 | all-reduce | flops 256 | bytes 2048 | tf_op jit(solution)/shard_map/psum | solution.py:84
  (184 shorter events, 270.7 us)
Async XLA Ops:
  7.2 347.3 %all-reduce.6.cloned.1.call-start = ((), (), s32[]{:S(2)}) async-start(), calls=%async_computation.2 | async-start | bytes 1048576 | tf_op jit(solution)/shard_map/psum | solution.py:30
  8.7 11.4 %collective-permute-start = (f32[384,256]{1,0:T(8,128)S(1)}, f32[384,256]{1,0:T(8,128)S(1)}, u32[]{:S(2)}, u32[]{:S(2)}) collective-permute-start(f32[384,256]{1,0:T(8,128)S(1)} %get-tuple-element.47), channel_id=1, source_target_pairs={{0,16},{16,32},{32,48},{48,64},{64,80},{80,96},{96,112},{1,17},{17... | collective-permute-start | bytes 1179656 | tf_op jit(solution)/shard_map/ppermute | solution.py:12
  15.2 11.0 %collective-permute-start.2 = (f32[384,256]{1,0:T(8,128)S(1)}, f32[384,256]{1,0:T(8,128)S(1)}, u32[]{:S(2)}, u32[]{:S(2)}) collective-permute-start(f32[384,256]{1,0:T(8,128)S(1)} %get-tuple-element.48), channel_id=1, source_target_pairs={{0,1},{1,2},{2,3},{3,4},{4,5},{5,6},{6,7},{7,8},{8,9},{9,10},{10,1... | collective-permute-start | bytes 1179656 | tf_op jit(solution)/shard_map/ppermute | solution.py:12
  18.8 11.5 %collective-permute-start.3 = (f32[384,256]{1,0:T(8,128)S(1)}, f32[384,256]{1,0:T(8,128)S(1)}, u32[]{:S(2)}, u32[]{:S(2)}) collective-permute-start(f32[384,256]{1,0:T(8,128)S(1)} %get-tuple-element.50), channel_id=1, source_target_pairs={{1,0},{2,1},{3,2},{4,3},{5,4},{6,5},{7,6},{8,7},{9,8},{10,9},{11,1... | collective-permute-start | bytes 1179656 | tf_op jit(solution)/shard_map/ppermute | solution.py:12
  51.4 11.8 %collective-permute-start.4 = (f32[384,256]{1,0:T(8,128)S(1)}, f32[384,256]{1,0:T(8,128)S(1)}, u32[]{:S(2)}, u32[]{:S(2)}) collective-permute-start(f32[384,256]{1,0:T(8,128)S(1)} %get-tuple-element.43), channel_id=1, source_target_pairs={{0,16},{16,32},{32,48},{48,64},{64,80},{80,96},{96,112},{1,17},{17... | collective-permute-start | bytes 1179656 | tf_op jit(solution)/shard_map/ppermute | solution.py:12
  58.5 9.6 collective-permute-start.6
  61.9 10.3 collective-permute-start.7
  110.4 13.3 %collective-permute-start.8 = (f32[384,256]{0,1:T(8,128)S(1)}, f32[384,256]{0,1:T(8,128)S(1)}, u32[]{:S(2)}, u32[]{:S(2)}) collective-permute-start(f32[384,256]{0,1:T(8,128)S(1)} %get-tuple-element.39), channel_id=1, source_target_pairs={{0,16},{16,32},{32,48},{48,64},{64,80},{80,96},{96,112},{1,17},{17... | collective-permute-start | bytes 1179656 | tf_op jit(solution)/shard_map/ppermute | solution.py:12
  157.2 13.7 %collective-permute-start.12 = (f32[384,256]{0,1:T(8,128)S(1)}, f32[384,256]{0,1:T(8,128)S(1)}, u32[]{:S(2)}, u32[]{:S(2)}) collective-permute-start(f32[384,256]{0,1:T(8,128)S(1)} %get-tuple-element.35), channel_id=1, source_target_pairs={{0,16},{16,32},{32,48},{48,64},{64,80},{80,96},{96,112},{1,17},{17... | collective-permute-start | bytes 1179656 | tf_op jit(solution)/shard_map/ppermute | solution.py:12
  356.8 20.3 %all-to-all-start = ((f32[128,4,256]{2,1,0:T(4,128)}), f32[128,4,256]{2,1,0:T(4,128)}, u32[]{:S(2)}, u32[]{:S(2)}) async-start(f32[128,4,256]{2,1,0:T(4,128)} %stack.114), calls=%async_computation | async-start | bytes 1048576 | tf_op jit(solution)/shard_map/all_to_all | solution.py:33
  364.0 511.7 %all-reduce.8.cloned.1.call-start = ((), (), s32[]{:S(2)}) async-start(), calls=%async_computation.3 | async-start | bytes 1048576 | tf_op jit(solution)/shard_map/psum | solution.py:30
  385.7 14.6 %collective-permute-start.16 = (f32[384,256]{0,1:T(8,128)}, f32[384,256]{0,1:T(8,128)}, u32[]{:S(2)}, u32[]{:S(2)}) collective-permute-start(f32[384,256]{0,1:T(8,128)} %get-tuple-element.31), channel_id=1, source_target_pairs={{0,16},{16,32},{32,48},{48,64},{64,80},{80,96},{96,112},{1,17},{17... | collective-permute-start | bytes 1179656 | tf_op jit(solution)/shard_map/ppermute | solution.py:12
  389.1 11.2 %collective-permute-start.17 = (f32[384,256]{0,1:T(8,128)}, f32[384,256]{0,1:T(8,128)}, u32[]{:S(2)}, u32[]{:S(2)}) collective-permute-start(f32[384,256]{0,1:T(8,128)} %get-tuple-element.34), channel_id=1, source_target_pairs={{16,0},{32,16},{48,32},{64,48},{80,64},{96,80},{112,96},{17,1},{33... | collective-permute-start | bytes 1179656 | tf_op jit(solution)/shard_map/ppermute | solution.py:12
  391.1 11.5 %collective-permute-start.18 = (f32[384,256]{0,1:T(8,128)}, f32[384,256]{0,1:T(8,128)}, u32[]{:S(2)}, u32[]{:S(2)}) collective-permute-start(f32[384,256]{0,1:T(8,128)} %get-tuple-element.33), channel_id=1, source_target_pairs={{0,1},{1,2},{2,3},{3,4},{4,5},{5,6},{6,7},{7,8},{8,9},{9,10},{10,1... | collective-permute-start | bytes 1179656 | tf_op jit(solution)/shard_map/ppermute | solution.py:12
  394.4 13.1 %collective-permute-start.19 = (f32[384,256]{0,1:T(8,128)}, f32[384,256]{0,1:T(8,128)}, u32[]{:S(2)}, u32[]{:S(2)}) collective-permute-start(f32[384,256]{0,1:T(8,128)} %get-tuple-element.32), channel_id=1, source_target_pairs={{1,0},{2,1},{3,2},{4,3},{5,4},{6,5},{7,6},{8,7},{9,8},{10,9},{11,1... | collective-permute-start | bytes 1179656 | tf_op jit(solution)/shard_map/ppermute | solution.py:12
  510.9 10.5 %collective-permute-start.22 = (f32[384,256]{0,1:T(8,128)S(1)}, f32[384,256]{0,1:T(8,128)S(1)}, u32[]{:S(2)}, u32[]{:S(2)}) collective-permute-start(f32[384,256]{0,1:T(8,128)S(1)} %get-tuple-element.29), channel_id=1, source_target_pairs={{0,1},{1,2},{2,3},{3,4},{4,5},{5,6},{6,7},{7,8},{8,9},{9,10},{10,1... | collective-permute-start | bytes 1179656 | tf_op jit(solution)/shard_map/ppermute | solution.py:12
  513.0 12.5 %collective-permute-start.23 = (f32[384,256]{0,1:T(8,128)S(1)}, f32[384,256]{0,1:T(8,128)S(1)}, u32[]{:S(2)}, u32[]{:S(2)}) collective-permute-start(f32[384,256]{0,1:T(8,128)S(1)} %get-tuple-element.28), channel_id=1, source_target_pairs={{1,0},{2,1},{3,2},{4,3},{5,4},{6,5},{7,6},{8,7},{9,8},{10,9},{11,1... | collective-permute-start | bytes 1179656 | tf_op jit(solution)/shard_map/ppermute | solution.py:12
  567.6 10.9 %collective-permute-start.26 = (f32[384,256]{0,1:T(8,128)S(1)}, f32[384,256]{0,1:T(8,128)S(1)}, u32[]{:S(2)}, u32[]{:S(2)}) collective-permute-start(f32[384,256]{0,1:T(8,128)S(1)} %get-tuple-element.25), channel_id=1, source_target_pairs={{0,1},{1,2},{2,3},{3,4},{4,5},{5,6},{6,7},{7,8},{8,9},{9,10},{10,1... | collective-permute-start | bytes 1179656 | tf_op jit(solution)/shard_map/ppermute | solution.py:12
  570.2 12.4 %collective-permute-start.27 = (f32[384,256]{0,1:T(8,128)S(1)}, f32[384,256]{0,1:T(8,128)S(1)}, u32[]{:S(2)}, u32[]{:S(2)}) collective-permute-start(f32[384,256]{0,1:T(8,128)S(1)} %get-tuple-element.24), channel_id=1, source_target_pairs={{1,0},{2,1},{3,2},{4,3},{5,4},{6,5},{7,6},{8,7},{9,8},{10,9},{11,1... | collective-permute-start | bytes 1179656 | tf_op jit(solution)/shard_map/ppermute | solution.py:12
  687.8 12.0 %collective-permute-start.31 = (f32[384,256]{0,1:T(8,128)S(1)}, f32[384,256]{0,1:T(8,128)S(1)}, u32[]{:S(2)}, u32[]{:S(2)}) collective-permute-start(f32[384,256]{0,1:T(8,128)S(1)} %get-tuple-element.20), channel_id=1, source_target_pairs={{1,0},{2,1},{3,2},{4,3},{5,4},{6,5},{7,6},{8,7},{9,8},{10,9},{11,1... | collective-permute-start | bytes 1179656 | tf_op jit(solution)/shard_map/ppermute | solution.py:12
  878.0 20.3 %all-to-all-start.1 = ((f32[128,4,256]{2,1,0:T(4,128)}), f32[128,4,256]{2,1,0:T(4,128)}, u32[]{:S(2)}, u32[]{:S(2)}) async-start(f32[128,4,256]{2,1,0:T(4,128)} %stack.135), calls=%async_computation.1 | async-start | bytes 1048576 | tf_op jit(solution)/shard_map/all_to_all | solution.py:33
  906.5 9.6 collective-permute-start.32
  911.8 10.4 %collective-permute-start.34 = (f32[384,256]{0,1:T(8,128)S(1)}, f32[384,256]{0,1:T(8,128)S(1)}, u32[]{:S(2)}, u32[]{:S(2)}) collective-permute-start(f32[384,256]{0,1:T(8,128)S(1)} %get-tuple-element.17), channel_id=1, source_target_pairs={{0,1},{1,2},{2,3},{3,4},{4,5},{5,6},{6,7},{7,8},{8,9},{9,10},{10,1... | collective-permute-start | bytes 1179656 | tf_op jit(solution)/shard_map/ppermute | solution.py:12
  914.5 11.9 %collective-permute-start.35 = (f32[384,256]{0,1:T(8,128)S(1)}, f32[384,256]{0,1:T(8,128)S(1)}, u32[]{:S(2)}, u32[]{:S(2)}) collective-permute-start(f32[384,256]{0,1:T(8,128)S(1)} %get-tuple-element.16), channel_id=1, source_target_pairs={{1,0},{2,1},{3,2},{4,3},{5,4},{6,5},{7,6},{8,7},{9,8},{10,9},{11,1... | collective-permute-start | bytes 1179656 | tf_op jit(solution)/shard_map/ppermute | solution.py:12
  (37 other events, 593.8 us)
Sparse Core Ops, SparseCore 0:
  203.9 150.5 all-reduce.5
  728.2 147.5 all-reduce.7
